TPU v7x, 32 devices: a whole 2x2x4 slice. The times are simulated.
32 devices in a mesh: group: 2 (over x), seq: 16 (over z, y, core).
Axes of the slice: x: 2, y: 2, z: 4, core: 2. Of those that a mesh axis runs over, the one named last changes fastest.
Arguments:
- query_rows: bfloat16 [8192, 1536], P(('group', 'seq')), parts along dimension 0, may hold values from -120 to 120
- key_rows: bfloat16 [8192, 1536], P(('group', 'seq')), parts along dimension 0, may hold values from -6.6 to 6.6
- value_rows: bfloat16 [8192, 1536], P(('group', 'seq')), parts along dimension 0, may hold values from -60 to 60
- block_list: int32 [64, 27], P(('group', 'seq')), parts along dimension 0, may hold values from -1 to 31, as said below
- out_weight: bfloat16 [1536, 3072], P('seq'), may hold values from -4 to 4
Outputs:
- projected: bfloat16 [8192, 3072], P(('group', 'seq')), parts along dimension 0
There are 2 independent parts, one for each index of `group`. A program takes and returns all parts, laid end to end along the dimension named above; an argument that names none is the same for every part. Nothing has to cross between parts.
Inputs may be any that keep to these rules, and one draw needn't show every extreme that they name: `block_list`: tile t lies at grid row (t // 2) // 8, grid column (t // 2) % 8 and frame group t % 2. Row t lists distinct key tiles whose grid row, grid column and frame group each differ from t's by at most one; every such tile that shares t's grid row or grid column is listed, t itself among them; the other slots hold -1.
All inputs are finite; a program needn't handle non-finite values.
Results may differ from a plain program's by a relative error of at most 0.0056.
Values may be sent and summed in bfloat16 or wider, within the bound.
A program may use at most 128 MiB of HBM per device.

v0:
```python
import math

import jax
import jax.numpy as jnp
from jax import lax
from jax.sharding import PartitionSpec as P

HD = 128
FRAMES = 2
GRID_COLS = 8


def shifted(value, axis, steps):
    count = lax.axis_size(axis)
    first, last = (max(0, -steps), min(count, count - steps))
    return lax.ppermute(value, axis, [(source, source + steps) for source in range(first, last)])


def body(query_rows, key_rows, value_rows, block_list, out_weight):
    row_count, features = query_rows.shape
    tile_rows = row_count // FRAMES
    head_count = features // HD
    scale = HD ** (-0.5)
    devices = lax.axis_size("seq")
    position = lax.axis_index("seq")
    columns_count = GRID_COLS
    key_value = jnp.stack([key_rows, value_rows])
    ordering = [
        -(columns_count + 1),
        -columns_count,
        -(columns_count - 1),
        -1,
        0,
        1,
        columns_count - 1,
        columns_count,
        columns_count + 1,
    ]
    received = {0: key_value}
    for offset in ordering:
        if offset != 0:
            received[offset] = shifted(key_value, "seq", offset)
    sources = position - jnp.array(ordering, dtype=jnp.int32)
    inside = (sources >= 0) & (sources < devices)
    tile_ids = sources[:, None] * FRAMES + jnp.arange(FRAMES, dtype=jnp.int32)[None, :]
    tile_ids = jnp.where(inside[:, None], tile_ids, -2).reshape(-1)
    member = jnp.any(block_list[:, :, None] == tile_ids[None, None, :], axis=1)
    allowed = jnp.repeat(jnp.repeat(member, tile_rows, axis=0), tile_rows, axis=1)
    per_block = math.gcd(head_count, 2)
    width = per_block * HD
    outputs = []
    for block in range(head_count // per_block):
        lower = block * width
        queries_here = query_rows[:, lower : lower + width].reshape(row_count, per_block, HD)
        keys_here = jnp.concatenate(
            [received[shift_by][0, :, lower : lower + width] for shift_by in ordering], axis=0
        )
        keys_here = keys_here.reshape(-1, per_block, HD)
        values_here = jnp.concatenate(
            [received[shift_by][1, :, lower : lower + width] for shift_by in ordering], axis=0
        )
        values_here = values_here.reshape(-1, per_block, HD)
        scores = (
            jnp.einsum("qhd,khd->hqk", queries_here, keys_here, preferred_element_type=jnp.float32)
            * scale
        )
        scores = jnp.where(allowed[None, :, :], scores, -jnp.inf)
        peak = jnp.max(scores, axis=-1, keepdims=True)
        weights = jnp.exp(scores - peak)
        totals = jnp.sum(weights, axis=-1, keepdims=True)
        probs = weights.astype(jnp.bfloat16)
        mixed = jnp.einsum("hqk,khd->qhd", probs, values_here, preferred_element_type=jnp.float32)
        mixed = mixed / jnp.transpose(totals, (1, 0, 2))
        outputs.append(mixed.astype(jnp.bfloat16).reshape(row_count, width))
    attention = jnp.concatenate(outputs, axis=1)
    summed = jnp.dot(
        attention,
        lax.all_gather(out_weight, "seq", axis=0, tiled=True),
        preferred_element_type=jnp.float32,
    )
    return summed.astype(jnp.bfloat16)


def solution(mesh):
    placed = (
        P(("group", "seq"), None),
        P(("group", "seq"), None),
        P(("group", "seq"), None),
        P(("group", "seq"), None),
        P("seq", None),
    )
    return jax.shard_map(
        body, mesh=mesh, in_specs=placed, out_specs=P(("group", "seq"), None), check_vma=False
    )
```

profile of v0, /device:TPU:25, one launch (start us, length us, event | category | flops | bytes accessed | tf_op | source)
XLA Modules:
  0.0 405.6 jit_solution(7567085291168828110)
XLA Ops:
  6.5 1.5 copy.142
  8.5 3.7 collective-permute-start
  12.2 2.4 collective-permute-start.1
  14.6 2.5 collective-permute-start.2
  17.1 2.6 collective-permute-start.3
  19.7 3.0 collective-permute-start.4
  24.2 0.8 fusion.104
  25.1 1.7 copy.148
  26.8 1.6 copy.228
  29.5 1.7 copy.229
  37.2 18.9 %collective-permute-done = bf16[2,256,1536]{1,2,0:T(8,128)(2,1)} collective-permute-done((bf16[2,256,1536]{1,2,0:T(8,128)(2,1)S(1)}, bf16[2,256,1536]{1,2,0:T(8,128)(2,1)}, u32[]{:S(2)}, u32[]{:S(2)}) %collective-permute-start) | collective-permute-done | bytes 1572896 | tf_op jit(solution)/shard_map/ppermute | solution.py:16
  56.0 1.3 collective-permute-start.5
  57.3 0.8 fusion.106
  58.2 38.9 %collective-permute-done.1 = bf16[2,256,1536]{1,2,0:T(8,128)(2,1)} collective-permute-done((bf16[2,256,1536]{1,2,0:T(8,128)(2,1)S(1)}, bf16[2,256,1536]{1,2,0:T(8,128)(2,1)}, u32[]{:S(2)}, u32[]{:S(2)}) %collective-permute-start.1) | collective-permute-done | bytes 1572896 | tf_op jit(solution)/shard_map/ppermute | solution.py:16
  97.0 1.3 collective-permute-start.6
  98.3 2.6 fusion.103
  100.9 29.8 %collective-permute-done.2 = bf16[2,256,1536]{1,2,0:T(8,128)(2,1)} collective-permute-done((bf16[2,256,1536]{1,2,0:T(8,128)(2,1)S(1)}, bf16[2,256,1536]{1,2,0:T(8,128)(2,1)}, u32[]{:S(2)}, u32[]{:S(2)}) %collective-permute-start.2) | collective-permute-done | bytes 1572896 | tf_op jit(solution)/shard_map/ppermute | solution.py:16
  130.8 1.5 collective-permute-start.7
  132.2 2.6 fusion.102
  134.9 1.6 copy.144
  136.5 1.7 copy.145
  138.2 2.6 fusion.101
  140.8 1.7 copy.146
  142.4 2.6 fusion.100
  145.0 1.7 copy.147
  146.6 2.6 fusion.99
  149.2 1.7 copy.149
  150.9 2.6 fusion.98
  153.5 1.7 copy.150
  155.1 2.6 fusion.97
  157.7 1.6 copy.151
  159.4 1.6 constant_dynamic-update-slice_fusion.8
  160.9 1.6 constant_dynamic-update-slice_fusion.17
  162.5 166.3 %collective-permute-done.7 = bf16[2,256,1536]{1,2,0:T(8,128)(2,1)S(1)} collective-permute-done((bf16[2,256,1536]{1,2,0:T(8,128)(2,1)S(1)}, bf16[2,256,1536]{1,2,0:T(8,128)(2,1)S(1)}, u32[]{:S(2)}, u32[]{:S(2)}) %collective-permute-start.7) | collective-permute-done | bytes 1572896 | tf_op jit(solution)/shard_map/ppermute | solution.py:16
  328.8 0.9 fusion.96
  332.8 1.7 copy.159
  355.0 1.7 copy.200
  362.0 1.0 copy.212
  366.8 1.0 fusion.93
  370.9 0.8 fusion.108
  372.3 0.9 fusion.90
  375.3 0.8 fusion.109
  376.1 0.9 fusion.16
  377.0 0.9 fusion.87
  381.5 0.9 fusion.84
  385.9 0.9 fusion.81
  390.3 0.9 fusion.78
  391.3 7.5 %convolution_convert_fusion = bf16[256,3072]{1,0:T(8,128)(2,1)} fusion(bf16[256,1536]{0,1:T(8,128)(2,1)S(1)} %constant_dynamic-update-slice_fusion.108, bf16[1536,3072]{1,0:T(8,128)(2,1)} %all-gather.2.cloned.1.call-done), kind=kOutput, calls=%fused_computation.36 | convolution fusion | flops 2416705536 | bytes 11796480 | tf_op jit(solution)/shard_map/dot_general | solution.py:76
  (484 shorter events, 56.5 us)
Async XLA Ops:
  6.5 384.7 %all-gather.2.cloned.1.call-start = ((), (), s32[]{:S(2)}) async-start(), calls=%async_computation | async-start | bytes 10027008 | tf_op jit(solution)/shard_map/all_gather | solution.py:78
  8.3 14.4 %copy-start.147 = (s32[9]{0:T(128)S(1)}, s32[9]{0:T(128)}, u32[]{:S(2)}) copy-start(s32[9]{0:T(128)} %constant.24) | copy-start | bytes 112
  8.5 47.6 %collective-permute-start = (bf16[2,256,1536]{1,2,0:T(8,128)(2,1)S(1)}, bf16[2,256,1536]{1,2,0:T(8,128)(2,1)}, u32[]{:S(2)}, u32[]{:S(2)}) collective-permute-start(bf16[2,256,1536]{1,2,0:T(8,128)(2,1)S(1)} %pad_maximum_fusion), channel_id=1, source_target_pairs={{9,0},{10,1},{11,2},{12,3},{13,4},{14,5},{15,6},{25,16},{26,17},{2... | collective-permute-start | bytes 4718600 | tf_op jit(solution)/shard_map/ppermute | solution.py:16
  12.2 84.9 %collective-permute-start.1 = (bf16[2,256,1536]{1,2,0:T(8,128)(2,1)S(1)}, bf16[2,256,1536]{1,2,0:T(8,128)(2,1)}, u32[]{:S(2)}, u32[]{:S(2)}) collective-permute-start(bf16[2,256,1536]{1,2,0:T(8,128)(2,1)S(1)} %pad_maximum_fusion), channel_id=1, source_target_pairs={{8,0},{9,1},{10,2},{11,3},{12,4},{13,5},{14,6},{15,7},{24,16},{25,... | collective-permute-start | bytes 4718600 | tf_op jit(solution)/shard_map/ppermute | solution.py:16
  14.6 116.1 %collective-permute-start.2 = (bf16[2,256,1536]{1,2,0:T(8,128)(2,1)S(1)}, bf16[2,256,1536]{1,2,0:T(8,128)(2,1)}, u32[]{:S(2)}, u32[]{:S(2)}) collective-permute-start(bf16[2,256,1536]{1,2,0:T(8,128)(2,1)S(1)} %pad_maximum_fusion), channel_id=1, source_target_pairs={{7,0},{8,1},{9,2},{10,3},{11,4},{12,5},{13,6},{14,7},{15,8},{23,16... | collective-permute-start | bytes 4718600 | tf_op jit(solution)/shard_map/ppermute | solution.py:16
  17.1 125.3 %collective-permute-start.3 = (bf16[2,256,1536]{1,2,0:T(8,128)(2,1)S(1)}, bf16[2,256,1536]{1,2,0:T(8,128)(2,1)}, u32[]{:S(2)}, u32[]{:S(2)}) collective-permute-start(bf16[2,256,1536]{1,2,0:T(8,128)(2,1)S(1)} %pad_maximum_fusion), channel_id=1, source_target_pairs={{1,0},{2,1},{3,2},{4,3},{5,4},{6,5},{7,6},{8,7},{9,8},{10,9},{11,1... | collective-permute-start | bytes 4718600 | tf_op jit(solution)/shard_map/ppermute | solution.py:16
  19.7 127.0 %collective-permute-start.4 = (bf16[2,256,1536]{1,2,0:T(8,128)(2,1)S(1)}, bf16[2,256,1536]{1,2,0:T(8,128)(2,1)}, u32[]{:S(2)}, u32[]{:S(2)}) collective-permute-start(bf16[2,256,1536]{1,2,0:T(8,128)(2,1)S(1)} %pad_maximum_fusion), channel_id=1, source_target_pairs={{0,1},{1,2},{2,3},{3,4},{4,5},{5,6},{6,7},{7,8},{8,9},{9,10},{10,1... | collective-permute-start | bytes 4718600 | tf_op jit(solution)/shard_map/ppermute | solution.py:16
  24.2 7.0 %copy-start.84 = (bf16[1,256,256]{1,2,0:T(8,128)(2,1)S(1)}, bf16[1,256,256]{1,2,0:T(8,128)(2,1)}, u32[]{:S(2)}) copy-start(bf16[1,256,256]{1,2,0:T(8,128)(2,1)} %get-tuple-element.110) | copy-start | bytes 393220
  56.0 94.8 %collective-permute-start.5 = (bf16[2,256,1536]{1,2,0:T(8,128)(2,1)S(1)}, bf16[2,256,1536]{1,2,0:T(8,128)(2,1)}, u32[]{:S(2)}, u32[]{:S(2)}) collective-permute-start(bf16[2,256,1536]{1,2,0:T(8,128)(2,1)S(1)} %pad_maximum_fusion), channel_id=1, source_target_pairs={{0,7},{1,8},{2,9},{3,10},{4,11},{5,12},{6,13},{7,14},{8,15},{16,23... | collective-permute-start | bytes 4718600 | tf_op jit(solution)/shard_map/ppermute | solution.py:16
  97.0 58.1 %collective-permute-start.6 = (bf16[2,256,1536]{1,2,0:T(8,128)(2,1)S(1)}, bf16[2,256,1536]{1,2,0:T(8,128)(2,1)}, u32[]{:S(2)}, u32[]{:S(2)}) collective-permute-start(bf16[2,256,1536]{1,2,0:T(8,128)(2,1)S(1)} %pad_maximum_fusion), channel_id=1, source_target_pairs={{0,8},{1,9},{2,10},{3,11},{4,12},{5,13},{6,14},{7,15},{16,24},{17,... | collective-permute-start | bytes 4718600 | tf_op jit(solution)/shard_map/ppermute | solution.py:16
  130.8 198.0 %collective-permute-start.7 = (bf16[2,256,1536]{1,2,0:T(8,128)(2,1)S(1)}, bf16[2,256,1536]{1,2,0:T(8,128)(2,1)S(1)}, u32[]{:S(2)}, u32[]{:S(2)}) collective-permute-start(bf16[2,256,1536]{1,2,0:T(8,128)(2,1)S(1)} %pad_maximum_fusion), channel_id=1, source_target_pairs={{0,9},{1,10},{2,11},{3,12},{4,13},{5,14},{6,15},{16,25},{17,26},{1... | collective-permute-start | bytes 4718600 | tf_op jit(solution)/shard_map/ppermute | solution.py:16
  329.7 5.5 %copy-start.79 = (bf16[1,256,256]{1,2,0:T(8,128)(2,1)S(1)}, bf16[1,256,256]{1,2,0:T(8,128)(2,1)}, u32[]{:S(2)}) copy-start(bf16[1,256,256]{1,2,0:T(8,128)(2,1)} %get-tuple-element.37) | copy-start | bytes 393220
  329.7 6.3 %copy-start.82 = (bf16[1,256,256]{1,2,0:T(8,128)(2,1)S(1)}, bf16[1,256,256]{1,2,0:T(8,128)(2,1)}, u32[]{:S(2)}) copy-start(bf16[1,256,256]{1,2,0:T(8,128)(2,1)} %get-tuple-element.25) | copy-start | bytes 393220
  329.7 7.0 %copy-start.86 = (bf16[1,256,256]{1,2,0:T(8,128)(2,1)S(1)}, bf16[1,256,256]{1,2,0:T(8,128)(2,1)}, u32[]{:S(2)}) copy-start(bf16[1,256,256]{1,2,0:T(8,128)(2,1)} %get-tuple-element.13) | copy-start | bytes 393220
  329.7 7.8 %copy-start.50 = (bf16[1,256,256]{1,2,0:T(8,128)(2,1)S(1)}, bf16[1,256,256]{1,2,0:T(8,128)(2,1)}, u32[]{:S(2)}) copy-start(bf16[1,256,256]{1,2,0:T(8,128)(2,1)} %get-tuple-element.95) | copy-start | bytes 393220
  330.5 7.8 %copy-start.56 = (bf16[1,256,256]{1,2,0:T(8,128)(2,1)S(1)}, bf16[1,256,256]{1,2,0:T(8,128)(2,1)}, u32[]{:S(2)}) copy-start(bf16[1,256,256]{1,2,0:T(8,128)(2,1)} %get-tuple-element.83) | copy-start | bytes 393220
  331.3 7.8 %copy-start.62 = (bf16[1,256,256]{1,2,0:T(8,128)(2,1)S(1)}, bf16[1,256,256]{1,2,0:T(8,128)(2,1)}, u32[]{:S(2)}) copy-start(bf16[1,256,256]{1,2,0:T(8,128)(2,1)} %get-tuple-element.71) | copy-start | bytes 393220
  332.0 7.8 %copy-start.68 = (bf16[1,256,256]{1,2,0:T(8,128)(2,1)S(1)}, bf16[1,256,256]{1,2,0:T(8,128)(2,1)}, u32[]{:S(2)}) copy-start(bf16[1,256,256]{1,2,0:T(8,128)(2,1)} %get-tuple-element.59) | copy-start | bytes 393220
  332.8 7.8 %copy-start.73 = (bf16[1,256,256]{1,2,0:T(8,128)(2,1)S(1)}, bf16[1,256,256]{1,2,0:T(8,128)(2,1)}, u32[]{:S(2)}) copy-start(bf16[1,256,256]{1,2,0:T(8,128)(2,1)} %get-tuple-element.47) | copy-start | bytes 393220
  334.5 6.8 %copy-start.77 = (bf16[1,256,256]{1,2,0:T(8,128)(2,1)S(1)}, bf16[1,256,256]{1,2,0:T(8,128)(2,1)}, u32[]{:S(2)}) copy-start(bf16[1,256,256]{1,2,0:T(8,128)(2,1)} %get-tuple-element.35) | copy-start | bytes 393220
  335.2 6.8 %copy-start.80 = (bf16[1,256,256]{1,2,0:T(8,128)(2,1)S(1)}, bf16[1,256,256]{1,2,0:T(8,128)(2,1)}, u32[]{:S(2)}) copy-start(bf16[1,256,256]{1,2,0:T(8,128)(2,1)} %get-tuple-element.23) | copy-start | bytes 393220
  336.0 6.8 %copy-start.83 = (bf16[1,256,256]{1,2,0:T(8,128)(2,1)S(1)}, bf16[1,256,256]{1,2,0:T(8,128)(2,1)}, u32[]{:S(2)}) copy-start(bf16[1,256,256]{1,2,0:T(8,128)(2,1)} %get-tuple-element.11) | copy-start | bytes 393220
  336.8 6.8 %copy-start.46 = (bf16[1,256,256]{1,2,0:T(8,128)(2,1)S(1)}, bf16[1,256,256]{1,2,0:T(8,128)(2,1)}, u32[]{:S(2)}) copy-start(bf16[1,256,256]{1,2,0:T(8,128)(2,1)} %get-tuple-element.93) | copy-start | bytes 393220
  337.5 6.8 %copy-start.51 = (bf16[1,256,256]{1,2,0:T(8,128)(2,1)S(1)}, bf16[1,256,256]{1,2,0:T(8,128)(2,1)}, u32[]{:S(2)}) copy-start(bf16[1,256,256]{1,2,0:T(8,128)(2,1)} %get-tuple-element.81) | copy-start | bytes 393220
  338.3 6.8 %copy-start.57 = (bf16[1,256,256]{1,2,0:T(8,128)(2,1)S(1)}, bf16[1,256,256]{1,2,0:T(8,128)(2,1)}, u32[]{:S(2)}) copy-start(bf16[1,256,256]{1,2,0:T(8,128)(2,1)} %get-tuple-element.69) | copy-start | bytes 393220
  339.0 6.8 %copy-start.63 = (bf16[1,256,256]{1,2,0:T(8,128)(2,1)S(1)}, bf16[1,256,256]{1,2,0:T(8,128)(2,1)}, u32[]{:S(2)}) copy-start(bf16[1,256,256]{1,2,0:T(8,128)(2,1)} %get-tuple-element.57) | copy-start | bytes 393220
  339.8 6.8 %copy-start.69 = (bf16[1,256,256]{1,2,0:T(8,128)(2,1)S(1)}, bf16[1,256,256]{1,2,0:T(8,128)(2,1)}, u32[]{:S(2)}) copy-start(bf16[1,256,256]{1,2,0:T(8,128)(2,1)} %get-tuple-element.45) | copy-start | bytes 393220
  340.6 6.8 %copy-start.74 = (bf16[1,256,256]{1,2,0:T(8,128)(2,1)S(1)}, bf16[1,256,256]{1,2,0:T(8,128)(2,1)}, u32[]{:S(2)}) copy-start(bf16[1,256,256]{1,2,0:T(8,128)(2,1)} %get-tuple-element.33) | copy-start | bytes 393220
  341.3 6.8 %copy-start.78 = (bf16[1,256,256]{1,2,0:T(8,128)(2,1)S(1)}, bf16[1,256,256]{1,2,0:T(8,128)(2,1)}, u32[]{:S(2)}) copy-start(bf16[1,256,256]{1,2,0:T(8,128)(2,1)} %get-tuple-element.21) | copy-start | bytes 393220
  342.1 6.8 %copy-start.81 = (bf16[1,256,256]{1,2,0:T(8,128)(2,1)S(1)}, bf16[1,256,256]{1,2,0:T(8,128)(2,1)}, u32[]{:S(2)}) copy-start(bf16[1,256,256]{1,2,0:T(8,128)(2,1)} %get-tuple-element.9) | copy-start | bytes 393220
  342.8 6.8 %copy-start.43 = (bf16[1,256,256]{1,2,0:T(8,128)(2,1)S(1)}, bf16[1,256,256]{1,2,0:T(8,128)(2,1)}, u32[]{:S(2)}) copy-start(bf16[1,256,256]{1,2,0:T(8,128)(2,1)} %get-tuple-element.91) | copy-start | bytes 393220
  343.6 6.8 %copy-start.47 = (bf16[1,256,256]{1,2,0:T(8,128)(2,1)S(1)}, bf16[1,256,256]{1,2,0:T(8,128)(2,1)}, u32[]{:S(2)}) copy-start(bf16[1,256,256]{1,2,0:T(8,128)(2,1)} %get-tuple-element.79) | copy-start | bytes 393220
  344.3 6.8 %copy-start.52 = (bf16[1,256,256]{1,2,0:T(8,128)(2,1)S(1)}, bf16[1,256,256]{1,2,0:T(8,128)(2,1)}, u32[]{:S(2)}) copy-start(bf16[1,256,256]{1,2,0:T(8,128)(2,1)} %get-tuple-element.67) | copy-start | bytes 393220
  345.1 6.8 %copy-start.59 = (bf16[1,256,256]{1,2,0:T(8,128)(2,1)S(1)}, bf16[1,256,256]{1,2,0:T(8,128)(2,1)}, u32[]{:S(2)}) copy-start(bf16[1,256,256]{1,2,0:T(8,128)(2,1)} %get-tuple-element.55) | copy-start | bytes 393220
  345.9 6.8 %copy-start.65 = (bf16[1,256,256]{1,2,0:T(8,128)(2,1)S(1)}, bf16[1,256,256]{1,2,0:T(8,128)(2,1)}, u32[]{:S(2)}) copy-start(bf16[1,256,256]{1,2,0:T(8,128)(2,1)} %get-tuple-element.43) | copy-start | bytes 393220
  346.6 6.8 %copy-start.70 = (bf16[1,256,256]{1,2,0:T(8,128)(2,1)S(1)}, bf16[1,256,256]{1,2,0:T(8,128)(2,1)}, u32[]{:S(2)}) copy-start(bf16[1,256,256]{1,2,0:T(8,128)(2,1)} %get-tuple-element.31) | copy-start | bytes 393220
  347.4 6.8 %copy-start.75 = (bf16[1,256,256]{1,2,0:T(8,128)(2,1)S(1)}, bf16[1,256,256]{1,2,0:T(8,128)(2,1)}, u32[]{:S(2)}) copy-start(bf16[1,256,256]{1,2,0:T(8,128)(2,1)} %get-tuple-element.19) | copy-start | bytes 393220
  348.9 7.8 %copy-start.41 = (bf16[1,256,256]{1,2,0:T(8,128)(2,1)S(1)}, bf16[1,256,256]{1,2,0:T(8,128)(2,1)}, u32[]{:S(2)}) copy-start(bf16[1,256,256]{1,2,0:T(8,128)(2,1)} %get-tuple-element.89) | copy-start | bytes 393220
  349.7 7.8 %copy-start.44 = (bf16[1,256,256]{1,2,0:T(8,128)(2,1)S(1)}, bf16[1,256,256]{1,2,0:T(8,128)(2,1)}, u32[]{:S(2)}) copy-start(bf16[1,256,256]{1,2,0:T(8,128)(2,1)} %get-tuple-element.77) | copy-start | bytes 393220
  350.4 7.8 %copy-start.48 = (bf16[1,256,256]{1,2,0:T(8,128)(2,1)S(1)}, bf16[1,256,256]{1,2,0:T(8,128)(2,1)}, u32[]{:S(2)}) copy-start(bf16[1,256,256]{1,2,0:T(8,128)(2,1)} %get-tuple-element.65) | copy-start | bytes 393220
  351.2 7.8 %copy-start.54 = (bf16[1,256,256]{1,2,0:T(8,128)(2,1)S(1)}, bf16[1,256,256]{1,2,0:T(8,128)(2,1)}, u32[]{:S(2)}) copy-start(bf16[1,256,256]{1,2,0:T(8,128)(2,1)} %get-tuple-element.53) | copy-start | bytes 393220
  351.9 7.8 %copy-start.60 = (bf16[1,256,256]{1,2,0:T(8,128)(2,1)S(1)}, bf16[1,256,256]{1,2,0:T(8,128)(2,1)}, u32[]{:S(2)}) copy-start(bf16[1,256,256]{1,2,0:T(8,128)(2,1)} %get-tuple-element.41) | copy-start | bytes 393220
  352.7 7.8 %copy-start.66 = (bf16[1,256,256]{1,2,0:T(8,128)(2,1)S(1)}, bf16[1,256,256]{1,2,0:T(8,128)(2,1)}, u32[]{:S(2)}) copy-start(bf16[1,256,256]{1,2,0:T(8,128)(2,1)} %get-tuple-element.29) | copy-start | bytes 393220
  353.5 7.8 %copy-start.71 = (bf16[1,256,256]{1,2,0:T(8,128)(2,1)S(1)}, bf16[1,256,256]{1,2,0:T(8,128)(2,1)}, u32[]{:S(2)}) copy-start(bf16[1,256,256]{1,2,0:T(8,128)(2,1)} %get-tuple-element.17) | copy-start | bytes 393220
  355.0 8.1 %copy-start = (bf16[2304,2,128]{0,2,1:T(8,128)(2,1)S(1)}, bf16[2304,2,128]{0,2,1:T(8,128)(2,1)}, u32[]{:S(2)}) copy-start(bf16[2304,2,128]{0,2,1:T(8,128)(2,1)} %constant_dynamic-update-slice_fusion.8) | copy-start | bytes 3538948
  355.0 8.1 %copy-start.42 = (bf16[1,256,256]{1,2,0:T(8,128)(2,1)S(1)}, bf16[1,256,256]{1,2,0:T(8,128)(2,1)}, u32[]{:S(2)}) copy-start(bf16[1,256,256]{1,2,0:T(8,128)(2,1)} %get-tuple-element.88) | copy-start | bytes 393220
  356.7 6.4 %copy-start.45 = (bf16[1,256,256]{1,2,0:T(8,128)(2,1)S(1)}, bf16[1,256,256]{1,2,0:T(8,128)(2,1)}, u32[]{:S(2)}) copy-start(bf16[1,256,256]{1,2,0:T(8,128)(2,1)} %get-tuple-element.76) | copy-start | bytes 393220
  357.5 5.7 %copy-start.49 = (bf16[1,256,256]{1,2,0:T(8,128)(2,1)S(1)}, bf16[1,256,256]{1,2,0:T(8,128)(2,1)}, u32[]{:S(2)}) copy-start(bf16[1,256,256]{1,2,0:T(8,128)(2,1)} %get-tuple-element.64) | copy-start | bytes 393220
  (109 other events, 139.3 us)
Sparse Core Ops, SparseCore 0:
  22.8 199.0 all-gather.1
where the time goes:
time: 407 us; the launch traced here: 406 us
  waiting for transfers between devices  254 us (62%)
  local copies, waits for them, and re-layouts  96 us (24%)
  starting transfers between devices  18.2 us (4%)
  matrix products  17.8 us (4%)
  between operations  15.2 us (4%)
  other arithmetic  4.45 us (1%)
    ppermute x8, waiting for transfers between devices, shifted(): lax.ppermute(value, axis, [(source, source + steps) for source in range(f...  254 us
    concatenate x60, local copies, waits for them, and re-layouts, body(): jnp.concatenate([received[shift_by][0, :, lower:lower + width] for shift_...  50.2 us
    unnamed x408, local copies, waits for them, and re-layouts  24 us
    slice x9, local copies, waits for them, and re-layouts, body(): received[shift_by][0, :, lower:lower + width]  19.8 us
    ppermute x8, starting transfers between devices, shifted(): lax.ppermute(value, axis, [(source, source + steps) for source in range(f...  18.2 us
  transfers between devices with their start and end apart: 9, of which 4 were waited for; matrix products, arithmetic and copies ran while one was open for 24% of the time, Pallas kernels for 0%

commit v1 on v0

v1 whole, which is shorter than its diff:
```python
import functools
import math

import jax
import jax.numpy as jnp
from jax import lax
from jax.experimental import pallas as pl
from jax.experimental.pallas import tpu as pltpu
from jax.sharding import PartitionSpec as P

HD = 128
FRAMES = 2
GRID_COLS = 8
MESH = pl.DeviceIdType.MESH
AHEAD = 2


def plan_of(n):
    rows = n // GRID_COLS
    verticals = 0 if rows <= 1 else (1 if rows == 2 else 2)
    return rows, verticals


def attend(q, keys, values, bias, scale):
    rows = q.shape[0]
    scores = jnp.concatenate(
        [
            lax.dot_general(q, k, (((1,), (1,)), ((), ())), preferred_element_type=jnp.float32)
            for k in keys
        ],
        axis=1,
    )
    scores = (scores.reshape(FRAMES, rows // FRAMES, -1) + bias[:, None, :]).reshape(rows, -1)
    peak = jnp.max(scores, axis=1, keepdims=True)
    weights = jnp.exp2((scores - peak) * (scale * math.log2(math.e)))
    totals = jnp.sum(weights, axis=1, keepdims=True)
    probs = weights.astype(jnp.bfloat16)
    mixed = None
    size = values[0].shape[0]
    for i, v in enumerate(values):
        part = jnp.dot(
            probs[:, i * size : (i + 1) * size], v, preferred_element_type=jnp.float32
        )
        mixed = part if mixed is None else mixed + part
    return (mixed / totals).astype(jnp.bfloat16)


def kernel(n, groups, chunks, gather, *refs):
    if gather:
        (q_ref, k_ref, v_ref, list_ref, w_ref, out_ref, wide_ref, kb, vb, bias_ref,
         vs, vr, hs, hr, zs, zr, ys, yr, xs, xr, cs, cr, local_sem) = refs
    else:
        (q_ref, k_ref, v_ref, list_ref, out_ref, kb, vb, bias_ref, vs, vr, hs, hr) = refs
    me = lax.axis_index("seq")
    mine = lax.axis_index("group")
    rows, verticals = plan_of(n)
    row, col = me // GRID_COLS, me % GRID_COLS
    row_count, features = q_ref.shape
    width = features // chunks
    heads_here = width // HD

    def when(condition):
        if condition is None:
            return lambda f: f()
        return pl.when(condition)

    def both(a, b):
        if a is None:
            return b
        if b is None:
            return a
        return jnp.logical_and(a, b)

    if verticals == 1:
        vertical = [((me + GRID_COLS) % n, None, (me + GRID_COLS) % n, None)]
    elif verticals == 2:
        vertical = [
            (me + GRID_COLS, row < rows - 1, me - GRID_COLS, row > 0),
            (me - GRID_COLS, row > 0, me + GRID_COLS, row < rows - 1),
        ]
    else:
        vertical = []
    has_left, has_right = col > 0, col < GRID_COLS - 1
    sides = [(me + 1, has_right, me - 1, has_left), (me - 1, has_left, me + 1, has_right)]

    def slot(side, e):
        return verticals + side * (1 + verticals) + e

    def columns(g):
        return pl.ds(pl.multiple_of(g * width, width), width)

    def vcopy(d, kv, g):
        src, buf = ((k_ref, kb), (v_ref, vb))[kv]
        return pltpu.make_async_remote_copy(
            src_ref=src.at[:, columns(g)],
            dst_ref=buf.at[d, :, columns(g)],
            send_sem=vs.at[d, kv, g],
            recv_sem=vr.at[d, kv, g],
            device_id=(mine, vertical[d][0]),
            device_id_type=MESH,
        )

    def hcopy(side, e, kv, g):
        src, buf = ((k_ref, kb), (v_ref, vb))[kv]
        source = src.at[:, columns(g)] if e == 0 else buf.at[e - 1, :, columns(g)]
        return pltpu.make_async_remote_copy(
            src_ref=source,
            dst_ref=buf.at[slot(side, e), :, columns(g)],
            send_sem=hs.at[side, e, kv, g],
            recv_sem=hr.at[side, e, kv, g],
            device_id=(mine, sides[side][0]),
            device_id_type=MESH,
        )

    if gather:
        outer_count = n // 4
        outer, middle, core = me // 4, (me // 2) % 2, me % 2
        y_peer = outer * 4 + (1 - middle) * 2 + core
        c_peer = outer * 4 + middle * 2 + (1 - core)
        part = w_ref.shape[1] // groups
        names = [(0, 0)] + [(s, d) for s in range(1, outer_count) for d in (0, 1)]
        index_of = {name: i for i, name in enumerate(names)}

        def where_from(name):
            s, d = name
            return outer - s if d == 0 else outer + s

        def exists(name):
            s, d = name
            if s == 0:
                return None
            return outer >= s if d == 0 else outer + s < outer_count

        def cols_of(g):
            return pl.ds(pl.multiple_of(g * part, 128), part)

        def block(name, other, core_there, g):
            m = 1 - middle if other else middle
            return wide_ref.at[where_from(name) * 4 + m * 2 + core_there, :, cols_of(g)]

        def zcopy(name):
            s, d = name
            to = me + 4 if d == 0 else me - 4
            arrives = index_of[(s + 1, d)]
            source = w_ref.at[:, cols_of(mine)] if s == 0 else block(name, False, core, mine)
            return pltpu.make_async_remote_copy(
                src_ref=source,
                dst_ref=block(name, False, core, mine),
                send_sem=zs.at[arrives],
                recv_sem=zr.at[arrives],
                device_id=(mine, to),
                device_id_type=MESH,
            )

        def ycopy(name):
            i = index_of[name]
            source = w_ref.at[:, cols_of(mine)] if name[0] == 0 else block(name, False, core, mine)
            return pltpu.make_async_remote_copy(
                src_ref=source, dst_ref=block(name, False, core, mine),
                send_sem=ys.at[i], recv_sem=yr.at[i],
                device_id=(mine, y_peer), device_id_type=MESH,
            )

        def xcopy(name, other, step):
            i = index_of[name]
            return pltpu.make_async_remote_copy(
                src_ref=block(name, other, core, mine), dst_ref=block(name, other, core, mine),
                send_sem=xs.at[int(other), i, step - 1], recv_sem=xr.at[int(other), i, step - 1],
                device_id=((mine + step) % groups, me), device_id_type=MESH,
            )

        def ccopy(name, other, step):
            i = index_of[name]
            g = (mine + groups - step) % groups
            if name[0] == 0 and not other:
                source, target = w_ref, wide_ref.at[me]
            else:
                source = target = block(name, other, core, g)
            return pltpu.make_async_remote_copy(
                src_ref=source, dst_ref=target,
                send_sem=cs.at[int(other), i, step], recv_sem=cr.at[int(other), i, step],
                device_id=(mine, c_peer), device_id_type=MESH,
            )

        started = []

        def launch(make, condition):
            started.append((make, condition))
            when(condition())(make().start)

        def can_pass(name):
            s, d = name
            return both(exists(name), outer < outer_count - 1 if d == 0 else outer > 0)

        def spread(name, other):
            ok = functools.partial(exists, name)
            for step in range(1, groups if name[0] > 0 or other else 1):
                launch(functools.partial(xcopy, name, other, step), ok)
            launch(functools.partial(ccopy, name, other, 0), ok)

        def arrived_z(name):
            when(exists(name))(zcopy_recv(name))
            if name[0] + 1 < outer_count:
                launch(functools.partial(zcopy, name), functools.partial(can_pass, name))
            launch(functools.partial(ycopy, name), functools.partial(exists, name))
            spread(name, False)

        def zcopy_recv(name):
            s, d = name
            copy = zcopy((s - 1, d))
            return copy.wait_recv

        def arrived_y(name):
            when(exists(name))(ycopy(name).wait_recv)
            spread(name, True)

        def arrived_x(name, other):
            for step in range(1, groups):
                when(exists(name))(xcopy(name, other, step).wait_recv)
                launch(
                    functools.partial(ccopy, name, other, step), functools.partial(exists, name)
                )

        def start_weights():
            for d in (0, 1):
                index_of[(0, d)] = 0
                if outer_count > 1:
                    launch(
                        functools.partial(zcopy, (0, d)), functools.partial(can_pass, (0, d))
                    )
            launch(functools.partial(ycopy, (0, 0)), lambda: None)
            spread((0, 0), False)

        def weight_slot(t):
            for d in (0, 1):
                if t + 1 < outer_count:
                    arrived_z((t + 1, d))
                if 1 <= t < outer_count:
                    arrived_y((t, d))
                if 2 <= t <= outer_count:
                    arrived_x((t - 1, d), False)
                if 3 <= t <= outer_count + 1:
                    arrived_x((t - 2, d), True)
            if t == 0:
                arrived_y((0, 0))
            if t == 1:
                arrived_x((0, 0), True)

        slots = outer_count + 2

    barrier = pltpu.get_barrier_semaphore()
    partners = []
    for to, sends, source, comes in vertical:
        partners.append(((mine, to), sends))
    for to, sends, source, comes in sides:
        partners.append(((mine, to), sends))
    if gather:
        partners.append(((mine, me + 4), outer < outer_count - 1))
        partners.append(((mine, me - 4), outer > 0))
        partners.append(((mine, y_peer), None))
        partners.append(((mine, c_peer), None))
        for step in range(1, groups):
            partners.append((((mine + step) % groups, me), None))
    for device, condition in partners:
        def greet(device=device):
            pl.semaphore_signal(barrier, inc=1, device_id=device, device_id_type=MESH)
        when(condition)(greet)
    expected = sum(
        1 if condition is None else condition.astype(jnp.int32) for device, condition in partners
    )
    pl.semaphore_wait(barrier, expected)

    def start_chunk(g):
        for kv in (0, 1):
            for d in range(verticals):
                when(vertical[d][1])(vcopy(d, kv, g).start)
        for side in (0, 1):
            for kv in (0, 1):
                when(sides[side][1])(hcopy(side, 0, kv, g).start)

    if gather:
        own_copy = pltpu.make_async_copy(w_ref, wide_ref.at[me], local_sem)
        own_copy.start()
        start_weights()
    for g in range(min(AHEAD, chunks)):
        start_chunk(g)

    for side in (0, 1):
        for e in range(1 + verticals):
            there = sides[side][3]
            if e > 0:
                there = both(there, vertical[e - 1][3])

            def clear(at=slot(side, e)):
                kb[at] = jnp.zeros(kb.shape[1:], kb.dtype)
                vb[at] = jnp.zeros(vb.shape[1:], vb.dtype)
            pl.when(jnp.logical_not(there))(clear)
    for d in range(verticals):
        if vertical[d][3] is not None:
            def clear_v(at=d):
                kb[at] = jnp.zeros(kb.shape[1:], kb.dtype)
                vb[at] = jnp.zeros(vb.shape[1:], vb.dtype)
            pl.when(jnp.logical_not(vertical[d][3]))(clear_v)

    tile_rows = row_count // FRAMES
    half = lax.broadcasted_iota(jnp.int32, (FRAMES, row_count), 1) // tile_rows
    order = [(e, s) for e in range(1 + verticals) for s in (None, 0, 1)]
    pieces = []
    for e, s in order:
        place, there = me, None
        if e > 0:
            place, there = vertical[e - 1][2], vertical[e - 1][3]
        if s is not None:
            place = place - 1 if s == 0 else place + 1
            there = both(there, sides[s][3])
        base = place * FRAMES
        if there is not None:
            base = jnp.where(there, base, -2 * FRAMES)
        pieces.append(half + base)
    ids = jnp.concatenate(pieces, axis=1)
    listed = list_ref[...]
    member = jnp.zeros(ids.shape, jnp.bool_)
    for j in range(listed.shape[1]):
        member = jnp.logical_or(member, ids == listed[:, j : j + 1])
    bias_ref[...] = jnp.where(member, 0.0, -jnp.inf)
    scale = HD ** (-0.5)

    def compute(g):
        def head(j, carry):
            at = pl.ds(pl.multiple_of(g * width + j * HD, HD), HD)

            def pick(own, buf, e, s):
                if s is None:
                    return own[:, at] if e == 0 else buf[e - 1, :, at]
                return buf[slot(s, e), :, at]

            out_ref[:, at] = attend(
                q_ref[:, at],
                [pick(k_ref, kb, e, s) for e, s in order],
                [pick(v_ref, vb, e, s) for e, s in order],
                bias_ref[...],
                scale,
            )
            return carry

        lax.fori_loop(0, heads_here, head, 0)

    def step(g, carry):
        @pl.when(g < chunks)
        def _():
            for d in range(verticals):
                for kv in (0, 1):
                    def relay(d=d, kv=kv):
                        vcopy(d, kv, g).wait_recv()
                        for side in (0, 1):
                            pl.when(sides[side][1])(hcopy(side, d + 1, kv, g).start)
                    when(vertical[d][3])(relay)

        @pl.when(g + AHEAD < chunks)
        def _():
            start_chunk(g + AHEAD)

        if gather:
            for t in range(slots):
                if t <= chunks:
                    pl.when(g == t)(functools.partial(weight_slot, t))

        @pl.when(g > 0)
        def _():
            for e in range(1 + verticals):
                for side in (0, 1):
                    there = sides[side][3]
                    if e > 0:
                        there = both(there, vertical[e - 1][3])
                    for kv in (0, 1):
                        pl.when(there)(hcopy(side, e, kv, g - 1).wait_recv)
            compute(g - 1)

        return carry

    lax.fori_loop(0, chunks + 1, step, 0)
    if gather:
        for t in range(chunks + 1, slots):
            weight_slot(t)

    def drain(g, carry):
        for kv in (0, 1):
            for d in range(verticals):
                when(vertical[d][1])(vcopy(d, kv, g).wait_send)
            for side in (0, 1):
                for e in range(1 + verticals):
                    goes = sides[side][1]
                    if e > 0:
                        goes = both(goes, vertical[e - 1][3])
                    when(goes)(hcopy(side, e, kv, g).wait_send)
        return carry

    lax.fori_loop(0, chunks, drain, 0)
    if gather:
        for name in names:
            for other in (False, True):
                for s in range(groups if name[0] > 0 or other else 1):
                    when(exists(name))(ccopy(name, other, s).wait_recv)
        for make, condition in started:
            when(condition())(make().wait_send)
        own_copy.wait()


def body(mesh, query_rows, key_rows, value_rows, block_list, out_weight):
    n, groups = mesh.shape["seq"], mesh.shape["group"]
    row_count, features = query_rows.shape
    head_count = features // HD
    chunks = head_count // math.gcd(head_count, 2)
    rows, verticals = plan_of(n)
    depth, model = out_weight.shape
    outer = n // 4
    gather = n % 4 == 0 and outer <= 4 and model % (128 * groups) == 0
    slots = 2 * (1 + verticals) + verticals
    vmem = pl.BlockSpec(memory_space=pltpu.VMEM)
    dma = pltpu.SemaphoreType.DMA
    blocks = 3 * (1 + verticals)
    args = [query_rows, key_rows, value_rows, block_list]
    out_shape = [jax.ShapeDtypeStruct((row_count, features), jnp.bfloat16)]
    out_specs = [vmem]
    scratch = [
        pltpu.VMEM((slots, row_count, features), jnp.bfloat16),
        pltpu.VMEM((slots, row_count, features), jnp.bfloat16),
        pltpu.VMEM((FRAMES, blocks * row_count), jnp.float32),
        dma((max(verticals, 1), 2, chunks)),
        dma((max(verticals, 1), 2, chunks)),
        dma((2, 1 + verticals, 2, chunks)),
        dma((2, 1 + verticals, 2, chunks)),
    ]
    if gather:
        count = 2 * outer - 1
        args.append(out_weight)
        out_shape.append(jax.ShapeDtypeStruct((n, depth, model), jnp.bfloat16))
        out_specs.append(pl.BlockSpec(memory_space=pl.ANY))
        scratch += [
            dma((count,)), dma((count,)),
            dma((count,)), dma((count,)),
            dma((2, count, max(groups - 1, 1))), dma((2, count, max(groups - 1, 1))),
            dma((2, count, groups)), dma((2, count, groups)),
            dma,
        ]
    results = pl.pallas_call(
        functools.partial(kernel, n, groups, chunks, gather),
        out_shape=out_shape,
        in_specs=[vmem] * len(args),
        out_specs=out_specs,
        scratch_shapes=scratch,
        compiler_params=pltpu.CompilerParams(collective_id=0, has_side_effects=True),
    )(*args)
    if gather:
        attention, wide = results
        wide = wide.reshape(n * depth, model)
    else:
        (attention,) = results
        wide = lax.all_gather(out_weight, "seq", axis=0, tiled=True)
    return jnp.dot(attention, wide, preferred_element_type=jnp.float32).astype(jnp.bfloat16)


def solution(mesh):
    placed = (
        P(("group", "seq"), None),
        P(("group", "seq"), None),
        P(("group", "seq"), None),
        P(("group", "seq"), None),
        P("seq", None),
    )
    return jax.shard_map(
        functools.partial(body, mesh),
        mesh=mesh,
        in_specs=placed,
        out_specs=P(("group", "seq"), None),
        check_vma=False,
    )
```

time: 407 us -> 135 us (0.33)
  the two profiles are of different devices: /device:TPU:25 before, /device:TPU:5 now
where the time goes in v1:
time: 135 us; the launch traced here: 134 us
  Pallas kernels  126 us (93%)
  matrix products  7.69 us (6%)
    pallas_call x1, Pallas kernels, body(): pl.pallas_call(functools.partial(kernel, n, groups, chunks, gather), out_...  126 us
    dot_general x1, matrix products, body(): jnp.dot(attention, wide, preferred_element_type=jnp.float32)  7.69 us

profile of v1, /device:TPU:5, one launch (start us, length us, event | category | flops | bytes accessed | tf_op | source)
XLA Modules:
  0.0 134.0 jit_solution(867971044059499880)
XLA Ops:
  0.0 126.3 %shard_map.55 = (bf16[256,1536]{1,0:T(8,128)(2,1)}, bf16[16,96,3072]{2,1,0:T(8,128)(2,1)}) custom-call(bf16[256,1536]{1,0:T(8,128)(2,1)} %refs_0_.1, bf16[256,1536]{1,0:T(8,128)(2,1)} %refs_1_.1, bf16[256,1536]{1,0:T(8,128)(2,1)} %refs_2_.1, s32[2,27]{1,0:T(2,128)} %refs_3_.1, bf16[96,3072]{1,0:T(8,128)(2,1)} %refs_4_.1), custom_call_target="tpu_custom_call" | custom-call | tf_op jit(solution)/shard_map/pallas_call | solution.py:446
  126.3 7.7 %convolution_convert_fusion = bf16[256,3072]{1,0:T(8,128)(2,1)} fusion(bf16[256,1536]{1,0:T(8,128)(2,1)} %get-tuple-element.7, bf16[1536,3072]{1,0:T(8,128)(2,1)} %bitcast.3), kind=kOutput, calls=%fused_computation | convolution fusion | flops 2416705536 | bytes 11796480 | tf_op jit(solution)/shard_map/dot_general | solution.py:460

commit v2 on v1

--- a/solution.py
+++ b/solution.py
@@ -12,7 +12,9 @@
 FRAMES = 2
 GRID_COLS = 8
 MESH = pl.DeviceIdType.MESH
-AHEAD = 2
+AHEAD = 1
+Z_AT, Y_AT, XZ_AT, XY_AT = (0, 2), (2, 2), (3, 2), (5, 2)
+Y_OWN, XY_OWN = 1, 4
 
 
 def plan_of(n):
@@ -232,21 +234,22 @@
             spread((0, 0), False)
 
         def weight_slot(t):
-            for d in (0, 1):
-                if t + 1 < outer_count:
-                    arrived_z((t + 1, d))
-                if 1 <= t < outer_count:
-                    arrived_y((t, d))
-                if 2 <= t <= outer_count:
-                    arrived_x((t - 1, d), False)
-                if 3 <= t <= outer_count + 1:
-                    arrived_x((t - 2, d), True)
-            if t == 0:
-                arrived_y((0, 0))
-            if t == 1:
-                arrived_x((0, 0), True)
-
-        slots = outer_count + 2
+            for s, d in names:
+                if s > 0 and t == Z_AT[0] + Z_AT[1] * (s - 1):
+                    arrived_z((s, d))
+            for s, d in names:
+                if t == (Y_AT[0] + Y_AT[1] * (s - 1) if s > 0 else Y_OWN):
+                    arrived_y((s, d))
+            for s, d in names:
+                if s > 0 and t == XZ_AT[0] + XZ_AT[1] * (s - 1):
+                    arrived_x((s, d), False)
+                if t == (XY_AT[0] + XY_AT[1] * (s - 1) if s > 0 else XY_OWN):
+                    arrived_x((s, d), True)
+
+        slots = 1 + max(
+            a + b * max(outer_count - 2, 0) for a, b in (Z_AT, Y_AT, XZ_AT, XY_AT)
+        )
+        slots = max(slots, Y_OWN + 1, XY_OWN + 1)
 
     barrier = pltpu.get_barrier_semaphore()
     partners = []
@@ -356,14 +359,14 @@
                             pl.when(sides[side][1])(hcopy(side, d + 1, kv, g).start)
                     when(vertical[d][3])(relay)
 
-        @pl.when(g + AHEAD < chunks)
-        def _():
-            start_chunk(g + AHEAD)
-
         if gather:
             for t in range(slots):
                 if t <= chunks:
                     pl.when(g == t)(functools.partial(weight_slot, t))
+
+        @pl.when(g + AHEAD < chunks)
+        def _():
+            start_chunk(g + AHEAD)
 
         @pl.when(g > 0)
         def _():
@@ -410,7 +413,7 @@
     n, groups = mesh.shape["seq"], mesh.shape["group"]
     row_count, features = query_rows.shape
     head_count = features // HD
-    chunks = head_count // math.gcd(head_count, 2)
+    chunks = head_count
     rows, verticals = plan_of(n)
     depth, model = out_weight.shape
     outer = n // 4

time: 135 us -> 117 us (0.87)
  Pallas kernels: 126 us -> 109 us
    pallas_call x1, Pallas kernels: 126 us -> 109 us  [body(): pl.pallas_call(functools.partial(kernel, n, groups, chunks, gather), out_...]
where the time goes in v2:
time: 117 us
  Pallas kernels  109 us (93%)
  matrix products  7.69 us (7%)
    pallas_call x1, Pallas kernels, body(): pl.pallas_call(functools.partial(kernel, n, groups, chunks, gather), out_...  109 us
    dot_general x1, matrix products, body(): jnp.dot(attention, wide, preferred_element_type=jnp.float32)  7.69 us

profile of v2, /device:TPU:5, one launch (start us, length us, event | category | flops | bytes accessed | tf_op | source)
XLA Modules:
  0.0 116.6 jit_solution(17813779000968909948)
XLA Ops:
  0.0 108.9 %shard_map.55 = (bf16[256,1536]{1,0:T(8,128)(2,1)}, bf16[16,96,3072]{2,1,0:T(8,128)(2,1)}) custom-call(bf16[256,1536]{1,0:T(8,128)(2,1)} %refs_0_.1, bf16[256,1536]{1,0:T(8,128)(2,1)} %refs_1_.1, bf16[256,1536]{1,0:T(8,128)(2,1)} %refs_2_.1, s32[2,27]{1,0:T(2,128)} %refs_3_.1, bf16[96,3072]{1,0:T(8,128)(2,1)} %refs_4_.1), custom_call_target="tpu_custom_call" | custom-call | tf_op jit(solution)/shard_map/pallas_call | solution.py:449
  109.0 7.7 %convolution_convert_fusion = bf16[256,3072]{1,0:T(8,128)(2,1)} fusion(bf16[256,1536]{1,0:T(8,128)(2,1)} %get-tuple-element.7, bf16[1536,3072]{1,0:T(8,128)(2,1)} %bitcast.3), kind=kOutput, calls=%fused_computation | convolution fusion | flops 2416705536 | bytes 11796480 | tf_op jit(solution)/shard_map/dot_general | solution.py:463

commit v3 on v2

--- a/solution.py
+++ b/solution.py
@@ -349,6 +349,11 @@
         lax.fori_loop(0, heads_here, head, 0)
 
     def step(g, carry):
+        if gather:
+            for t in range(slots):
+                if t <= chunks:
+                    pl.when(g == t)(functools.partial(weight_slot, t))
+
         @pl.when(g < chunks)
         def _():
             for d in range(verticals):
@@ -358,11 +363,6 @@
                         for side in (0, 1):
                             pl.when(sides[side][1])(hcopy(side, d + 1, kv, g).start)
                     when(vertical[d][3])(relay)
-
-        if gather:
-            for t in range(slots):
-                if t <= chunks:
-                    pl.when(g == t)(functools.partial(weight_slot, t))
 
         @pl.when(g + AHEAD < chunks)
         def _():

time: 117 us -> 120 us (1.026)
  Pallas kernels: 109 us -> 112 us
    pallas_call x1, Pallas kernels: 109 us -> 112 us  [body(): pl.pallas_call(functools.partial(kernel, n, groups, chunks, gather), out_...]
where the time goes in v3:
time: 120 us
  Pallas kernels  112 us (93%)
  matrix products  7.69 us (6%)
    pallas_call x1, Pallas kernels, body(): pl.pallas_call(functools.partial(kernel, n, groups, chunks, gather), out_...  112 us
    dot_general x1, matrix products, body(): jnp.dot(attention, wide, preferred_element_type=jnp.float32)  7.69 us

profile of v3, /device:TPU:5, one launch (start us, length us, event | category | flops | bytes accessed | tf_op | source)
XLA Modules:
  0.0 119.9 jit_solution(208353546862677871)
XLA Ops:
  0.0 112.2 %shard_map.55 = (bf16[256,1536]{1,0:T(8,128)(2,1)}, bf16[16,96,3072]{2,1,0:T(8,128)(2,1)}) custom-call(bf16[256,1536]{1,0:T(8,128)(2,1)} %refs_0_.1, bf16[256,1536]{1,0:T(8,128)(2,1)} %refs_1_.1, bf16[256,1536]{1,0:T(8,128)(2,1)} %refs_2_.1, s32[2,27]{1,0:T(2,128)} %refs_3_.1, bf16[96,3072]{1,0:T(8,128)(2,1)} %refs_4_.1), custom_call_target="tpu_custom_call" | custom-call | tf_op jit(solution)/shard_map/pallas_call | solution.py:449
  112.2 7.7 %convolution_convert_fusion = bf16[256,3072]{1,0:T(8,128)(2,1)} fusion(bf16[256,1536]{1,0:T(8,128)(2,1)} %get-tuple-element.7, bf16[1536,3072]{1,0:T(8,128)(2,1)} %bitcast.3), kind=kOutput, calls=%fused_computation | convolution fusion | flops 2416705536 | bytes 11796480 | tf_op jit(solution)/shard_map/dot_general | solution.py:463
